TPU v7x, 32 devices: a whole 2x2x4 slice. The times are simulated.
32 devices in a mesh: frames: 4 (over x, core), codes: 8 (over z, y).
Axes of the slice: x: 2, y: 2, z: 4, core: 2. Of those that a mesh axis runs over, the one named last changes fastest.
Arguments:
- hidden: bfloat16 [16384, 1024], P('frames'), may hold values from -5 to 5
- head: bfloat16 [1024, 8192], P('frames', 'codes'), may hold values from -2 to 2
- chosen: int32 [8, 16384], P(None, 'frames'), may hold values from 0 to 1023
Outputs:
- confidence: float32 [8, 16384], P(None, 'frames')
- entropy: float32 [8, 16384], P(None, 'frames')
All inputs are finite; a program needn't handle non-finite values.
Results may differ from a plain program's by a relative error of at most 0.0003.
Values may be sent and summed in bfloat16 or wider, within the bound.
No kernel may reach another device: no remote copies, remote signals or barrier semaphores. Data moves between devices by JAX's collectives and lax.ppermute only.
A program may use at most 64 MiB of HBM per device.

v0:
```python
import jax
import jax.numpy as jnp
from jax import lax
from jax.sharding import PartitionSpec as P

CODES = 1024


def partner(block, axis, bit):
    count = lax.axis_size(axis)
    route = []
    for low in range(count):
        high = low | 1 << bit
        if high != low and high < count:
            route += [(low, high), (high, low)]
    return lax.ppermute(block, axis, route)


def finish(top_score, exp_total, exp_logit, picked):
    log_total = top_score + jnp.log(exp_total)
    return (picked - log_total, log_total - exp_logit / exp_total)


def combine(earlier, later):
    highest = jnp.maximum(earlier[0], later[0])
    early_factor = jnp.exp(earlier[0] - highest)
    late_factor = jnp.exp(later[0] - highest)
    return (
        highest,
        earlier[1] * early_factor + later[1] * late_factor,
        earlier[2] * early_factor + later[2] * late_factor,
        earlier[3] + later[3],
    )


def on_device(hidden, head, chosen):
    row_count = hidden.shape[0]
    columns = head.shape[1]
    levels = chosen.shape[0]
    shard_index = lax.axis_index("codes")
    logits = jnp.dot(
        hidden,
        lax.all_gather(head, "frames", axis=0, tiled=True),
        preferred_element_type=jnp.float32,
    )
    group_count = max(columns // CODES, 1)
    level_span = min(columns, CODES)
    first_column = shard_index * columns
    first_level = first_column // CODES
    offset_code = first_column % CODES
    blocks = logits.reshape(row_count, group_count, level_span)
    local_max = jnp.max(blocks, axis=2)
    wanted = lax.dynamic_slice_in_dim(chosen, first_level, group_count, 0).T - offset_code
    matches = wanted[:, :, None] == lax.broadcasted_iota(jnp.int32, (1, 1, level_span), 2)
    picked = jnp.sum(jnp.where(matches, blocks, 0.0), axis=2)
    shifted = jnp.exp(blocks - local_max[:, :, None])
    local_total = jnp.sum(shifted, axis=2)
    local_logit = jnp.sum(shifted * blocks, axis=2)
    sharers = max(CODES // columns, 1)
    if sharers == 1:
        confidence, entropy = finish(local_max.T, local_total.T, local_logit.T, picked.T)
    else:
        current = (local_max[:, 0], local_total[:, 0], local_logit[:, 0], picked[:, 0])
        step_count = sharers.bit_length() - 1
        for step in range(step_count):
            bit_number = step_count - 1 - step
            my_bit = shard_index // 2**bit_number % 2
            halves = tuple((piece.reshape(2, piece.shape[0] // 2) for piece in current))
            keeping = tuple((jnp.where(my_bit == 0, part[0], part[1]) for part in halves))
            sending = tuple((jnp.where(my_bit == 0, part[1], part[0]) for part in halves))
            arrived = partner(sending, "codes", bit_number)
            current = combine(keeping, arrived)
        confidence, entropy = finish(
            current[0][None], current[1][None], current[2][None], current[3][None]
        )
    gathered = (
        lax.all_gather(confidence, "codes", axis=0, tiled=True),
        lax.all_gather(entropy, "codes", axis=0, tiled=True),
    )
    return (gathered[0].reshape(levels, row_count), gathered[1].reshape(levels, row_count))


def solution(mesh):
    placed = (P("frames", None), P("frames", "codes"), P(None, "frames"))
    return jax.shard_map(
        on_device,
        mesh=mesh,
        in_specs=placed,
        out_specs=(P(None, "frames"), P(None, "frames")),
        check_vma=False,
    )
```

profile of v0, /device:TPU:0, one launch (start us, length us, event | category | flops | bytes accessed | tf_op | source)
XLA Modules:
  0.0 129.0 jit_solution(15632191516104400551)
XLA Ops:
  7.2 0.0 all-gather.4.cloned.1.call-start
  7.2 0.7 all-gather.4.cloned.1.call-update
  7.9 0.9 dynamic-slice_subtract_fusion
  8.9 26.0 %all-gather.4.cloned.1.call-done = bf16[1024,1024]{1,0:T(8,128)(2,1)} async-done(((bf16[256,1024]{1,0:T(8,128)(2,1)}), bf16[1024,1024]{1,0:T(8,128)(2,1)}) %all-gather.4.cloned.1.call-update) | async-done | bytes 2097168 | tf_op jit(solution)/shard_map/all_gather | solution.py:43
  34.8 16.1 %fusion.2 = (f32[4096]{0:T(1024)S(1)}, f32[4096,1024]{0,1:T(8,128)}) fusion(bf16[4096,1024]{1,0:T(8,128)(2,1)} %param.3, bf16[1024,1024]{1,0:T(8,128)(2,1)} %all-gather.4.cloned.1.call-done), kind=kOutput, calls=%fused_computation.9 | convolution fusion | flops 8594124800 | bytes 27279360 | tf_op jit(solution)/shard_map/dot_general | solution.py:41
  51.0 8.7 %multiply_reduce_fusion = (f32[4096]{0:T(1024)S(1)}, f32[4096]{0:T(1024)S(1)}, f32[4096]{0:T(1024)S(1)}) fusion(f32[4096,1024]{0,1:T(8,128)} %get-tuple-element.8, f32[4096]{0:T(1024)S(1)} %get-tuple-element.7, s32[4096]{0:T(1024)S(1)} %bitcast.3), kind=kLoop, calls=%fused_computation | loop fusion | flops 29347840 | bytes 16859136 | tf_op jit(solution)/shard_map/reduce_sum | solution.py:58
  59.7 30.6 %all-gather = f32[32768]{0:T(1024)S(1)} all-gather(f32[4096]{0:T(1024)S(1)} %get-tuple-element.6), channel_id=2, replica_groups=mesh['frames'=4,'codes'=8] {'codes'}, dimensions={0}, use_global_device_ids=true | all-gather | bytes 147456 | tf_op jit(solution)/shard_map/all_gather | solution.py:77
  90.3 0.7 reshape.93
  91.0 30.5 %all-gather.1 = f32[32768]{0:T(1024)S(1)} all-gather(f32[4096]{0:T(1024)S(1)} %get-tuple-element.5), channel_id=3, replica_groups=mesh['frames'=4,'codes'=8] {'codes'}, dimensions={0}, use_global_device_ids=true | all-gather | bytes 147456 | tf_op jit(solution)/shard_map/all_gather | solution.py:78
  121.5 0.7 reshape.94
  (1 shorter events, 0.0 us)
Async XLA Ops:
  7.2 27.7 %all-gather.4.cloned.1.call-start = ((), (), s32[]{:S(2)}) async-start(), calls=%async_computation | async-start | bytes 2621440 | tf_op jit(solution)/shard_map/all_gather | solution.py:43
Sparse Core Ops, SparseCore 0:
  9.5 25.2 all-gather.3
where the time goes:
time: 129 us
  blocking collectives  61.1 us (47%)
  waiting for transfers between devices  26.7 us (21%)
  matrix products  16.1 us (12%)
  between operations  14.1 us (11%)
  other arithmetic  9.64 us (7%)
  local copies, waits for them, and re-layouts  1.37 us (1%)
    all_gather x1, blocking collectives, on_device(): lax.all_gather(confidence, 'codes', axis=0, tiled=True)  30.6 us
    all_gather x1, blocking collectives, on_device(): lax.all_gather(entropy, 'codes', axis=0, tiled=True)  30.5 us
    all_gather x1, waiting for transfers between devices, on_device(): lax.all_gather(head, 'frames', axis=0, tiled=True)  26 us
    dot_general x1, matrix products, on_device(): jnp.dot(hidden, lax.all_gather(head, 'frames', axis=0, tiled=True), prefe...  16.1 us
    reduce_sum x1, other arithmetic, on_device(): local_logit = jnp.sum(shifted * blocks, axis=2)  8.7 us
  transfers between devices with their start and end apart: 1, of which 1 were waited for; matrix products, arithmetic and copies ran while one was open for 1% of the time, Pallas kernels for 0%

commit v1 on v0

v1 whole, which is shorter than its diff:
```python
import functools

import jax
import jax.numpy as jnp
from jax import lax
from jax.experimental import pallas as pl
from jax.experimental.pallas import tpu as pltpu
from jax.sharding import PartitionSpec as P

CODES = 1024
TILE = 256
UNROLL = 4
SPLITS = (512, 512)
VMEM = pl.BlockSpec(memory_space=pltpu.VMEM)
SMEM = pl.BlockSpec(memory_space=pltpu.SMEM)


def flip(block, axis, bit):
    count = lax.axis_size(axis)
    return lax.ppermute(block, axis, [(i, i ^ 1 << bit) for i in range(count)])


def spread(pieces, axis, bits):
    for bit in bits:
        for offset in sorted(pieces):
            pieces[offset | 1 << bit] = flip(pieces[offset], axis, bit)
    return pieces


def in_vmem(shape, dtype):
    return pltpu.MemorySpace.VMEM(shape, dtype)


def partial_kernel(widths, place, hidden, own, sibling, *rest):
    outs, head_t = rest[:-1], rest[-1]
    rows = own.shape[0]
    core = place[0]
    head_t[:, pl.ds(pl.multiple_of(core * rows, rows), rows)] = own[...].T
    head_t[:, pl.ds(pl.multiple_of((1 - core) * rows, rows), rows)] = sibling[...].T
    span = 2 * rows
    depth = pl.ds(pl.multiple_of(place[1] * span, span), span)

    def body(step, carry):
        for lane in range(UNROLL):
            tile = pl.ds(pl.multiple_of((step * UNROLL + lane) * TILE, TILE), TILE)
            block = hidden[tile, depth]
            low = 0
            for out, width in zip(outs, widths):
                out[:, tile] = lax.dot_general(
                    head_t[low : low + width, :],
                    block,
                    (((1,), (1,)), ((), ())),
                    preferred_element_type=jnp.float32,
                )
                low += width
        return carry

    lax.fori_loop(0, hidden.shape[0] // (TILE * UNROLL), body, 0)


def partial_logits(place, hidden, own, sibling, widths):
    frames = hidden.shape[0]
    rows, columns = own.shape
    return pl.pallas_call(
        functools.partial(partial_kernel, widths),
        in_specs=[SMEM, VMEM, VMEM, VMEM],
        out_specs=[VMEM] * len(widths),
        out_shape=[pltpu.VMEM((width, frames), jnp.float32) for width in widths],
        scratch_shapes=[pltpu.VMEM((columns, 2 * rows), jnp.bfloat16)],
        compiler_params=pltpu.CompilerParams(vmem_limit_bytes=8 << 20),
        cost_estimate=pl.CostEstimate(
            flops=4 * frames * rows * columns, bytes_accessed=1 << 20, transcendentals=0
        ),
        name="partial",
    )(place, hidden, own, sibling)


def stats_kernel(pairs, first, last, base, place, hidden, part, chosen, *rest):
    pieces, rest = rest[: 2 * pairs], rest[2 * pairs :]
    before, rest = (None, rest) if first else (rest[0], rest[1:])
    out, head_t = rest
    rows, width = pieces[0].shape
    span = 2 * rows
    core = place[0]
    for pair in range(pairs):
        for side in range(2):
            spot = pl.multiple_of((core if side == 0 else 1 - core) * rows, rows)
            head_t[pair, :, pl.ds(spot, rows)] = pieces[2 * pair + side][...].T
    sublane = lax.broadcasted_iota(jnp.int32, (8, TILE), 0) + base

    def body(step, carry):
        for lane in range(UNROLL):
            tile = pl.ds(pl.multiple_of((step * UNROLL + lane) * TILE, TILE), TILE)
            logits = part[:, tile]
            for pair in range(pairs):
                depth = pl.ds(pl.multiple_of((place[1] ^ (pair + 1)) * span, span), span)
                logits = logits + lax.dot_general(
                    head_t[pair],
                    hidden[tile, depth],
                    (((1,), (1,)), ((), ())),
                    preferred_element_type=jnp.float32,
                )
            highest = jnp.max(logits, axis=0, keepdims=True)
            if not first:
                highest = jnp.maximum(highest, before[0:1, tile])
            wanted = chosen[pl.ds(place[2], 1), tile] - place[3] - sublane
            total = jnp.zeros((8, TILE), jnp.float32)
            weighted, picked = total, total
            for row in range(0, width, 8):
                piece = logits[row : row + 8]
                below = piece - highest
                power = jnp.exp(below)
                total += power
                weighted += power * below
                picked = jnp.where(wanted == row, piece, picked)
            total = jnp.sum(total, axis=0, keepdims=True)
            weighted = jnp.sum(weighted, axis=0, keepdims=True)
            picked = jnp.sum(picked, axis=0, keepdims=True)
            if not first:
                drop = before[0:1, tile] - highest
                factor = jnp.exp(drop)
                total += factor * before[1:2, tile]
                weighted += factor * (before[2:3, tile] + drop * before[1:2, tile])
                picked += before[3:4, tile]
            if last:
                log_total = jnp.log(total)
                out[0:1, tile] = picked - (highest + log_total)
                out[1:2, tile] = log_total - weighted / total
            else:
                out[0:1, tile] = highest
                out[1:2, tile] = total
                out[2:3, tile] = weighted
                out[3:4, tile] = picked
        return carry

    lax.fori_loop(0, hidden.shape[0] // (TILE * UNROLL), body, 0)


def chunk_stats(place, hidden, part, chosen, pieces, before, base, last):
    frames = hidden.shape[0]
    rows, width = pieces[0].shape
    pairs = len(pieces) // 2
    first = before is None
    args = [place, hidden, part, chosen, *pieces] + ([] if first else [before])
    return pl.pallas_call(
        functools.partial(stats_kernel, pairs, first, last, base),
        in_specs=[SMEM] + [VMEM] * (len(args) - 1),
        out_specs=VMEM,
        out_shape=jax.ShapeDtypeStruct((2 if last else 4, frames), jnp.float32),
        scratch_shapes=[pltpu.VMEM((pairs, width, 2 * rows), jnp.bfloat16)],
        compiler_params=pltpu.CompilerParams(vmem_limit_bytes=12 << 20),
        cost_estimate=pl.CostEstimate(
            flops=4 * pairs * frames * rows * width,
            bytes_accessed=1 << 20,
            transcendentals=frames * width,
        ),
        name="stats",
    )(*args)


def place_kernel(offsets, place, *refs):
    pieces, (confidence, entropy) = refs[:-2], refs[-2:]
    for offset, piece in zip(offsets, pieces):
        row = pl.ds(place[2] ^ offset, 1)
        confidence[row, :] = piece[0:1, :]
        entropy[row, :] = piece[1:2, :]


def put_in_place(place, pieces):
    offsets = sorted(pieces)
    shape = (len(offsets), pieces[0].shape[1])
    return pl.pallas_call(
        functools.partial(place_kernel, offsets),
        in_specs=[SMEM] + [VMEM] * len(offsets),
        out_specs=[VMEM, VMEM],
        out_shape=[jax.ShapeDtypeStruct(shape, jnp.float32)] * 2,
        compiler_params=pltpu.CompilerParams(vmem_limit_bytes=4 << 20),
        name="place",
    )(place, *(pieces[offset] for offset in offsets))


def combine(earlier, later):
    highest = jnp.maximum(earlier[0], later[0])
    early, late = earlier[0] - highest, later[0] - highest
    early_factor, late_factor = jnp.exp(early), jnp.exp(late)
    return (
        highest,
        early_factor * earlier[1] + late_factor * later[1],
        early_factor * (earlier[2] + early * earlier[1])
        + late_factor * (later[2] + late * later[1]),
        earlier[3] + later[3],
    )


def shared_levels(stats, sharers, levels):
    shard = lax.axis_index("codes")
    current = tuple(stats)
    for bit in reversed(range(sharers.bit_length() - 1)):
        mine = shard >> bit & 1
        halves = tuple(piece.reshape(2, -1) for piece in current)
        keep = tuple(jnp.where(mine == 0, half[0], half[1]) for half in halves)
        send = tuple(jnp.where(mine == 0, half[1], half[0]) for half in halves)
        current = combine(keep, tuple(flip(piece, "codes", bit) for piece in send))
    highest, total, weighted, picked = current
    log_total = jnp.log(total)
    results = (picked - (highest + log_total), log_total - weighted / total)
    return tuple(
        lax.all_gather(result, "codes", axis=0, tiled=True).reshape(levels, -1)
        for result in results
    )


def on_device(hidden, head, chosen):
    columns = head.shape[1]
    levels = chosen.shape[0]
    frame_count, code_count = lax.axis_size("frames"), lax.axis_size("codes")
    sharers = max(CODES // columns, 1)
    splits = SPLITS if sharers == 1 else (columns,)
    me, shard = lax.axis_index("frames"), lax.axis_index("codes")
    first_column = shard * columns
    place = jnp.stack([me & 1, me >> 1, first_column // CODES, first_column % CODES])
    place = place.astype(jnp.int32)
    far_bits = list(reversed(range(1, frame_count.bit_length() - 1)))

    chunks, low = [], 0
    for width in splits:
        chunks.append(head[:, low : low + width])
        low += width
    sibling = flip(head, "frames", 0)
    far = []
    for chunk in chunks:
        pieces = spread({0: chunk}, "frames", far_bits)
        del pieces[0]
        far.append(pieces)
    hidden = pltpu.with_memory_space_constraint(hidden, pltpu.VMEM)
    parts = partial_logits(place, hidden, head, sibling, splits)
    stats, base = None, 0
    for index, pieces in enumerate(far):
        ordered = []
        for offset in sorted(pieces):
            ordered += [pieces[offset], flip(pieces[offset], "frames", 0)]
        last = index == len(far) - 1 and sharers == 1
        stats = chunk_stats(
            place, hidden, parts[index], chosen, ordered, stats, base, last
        )
        base += splits[index]
    if sharers > 1:
        return shared_levels(stats, sharers, levels)
    bits = reversed(range(code_count.bit_length() - 1))
    return tuple(put_in_place(place, spread({0: stats}, "codes", bits)))


def solution(mesh):
    placed = (P("frames", None), P("frames", "codes"), P(None, "frames"))
    return jax.shard_map(
        on_device,
        mesh=mesh,
        in_specs=placed,
        out_specs=(P(None, "frames"), P(None, "frames")),
        check_vma=False,
    )
```

time: 129 us -> 56.1 us (0.43)
  blocking collectives: 61.1 us -> 0 us
  Pallas kernels: 0 us -> 19.6 us
  matrix products: 16.1 us -> 0 us
  starting transfers between devices: 0.04 us -> 13.7 us
  between operations: 14.1 us -> 0.71 us
  waiting for transfers between devices: 26.7 us -> 16.3 us
  other arithmetic: 9.64 us -> 0.08 us
  local copies, waits for them, and re-layouts: 1.37 us -> 5.49 us
    all_gather x2 -> x0, blocking collectives: 61.1 us -> none  [the longest x1 30.6 us: on_device(): lax.all_gather(confidence, 'codes', axis=0, tiled=True)]
    all_gather x1 -> x0, waiting for transfers between devices: 26 us -> none  [on_device(): lax.all_gather(head, 'frames', axis=0, tiled=True)]
    pallas_call x0 -> x4, Pallas kernels: none -> 19.6 us  [the longest x2 12.2 us: chunk_stats(): pl.pallas_call(functools.partial(stats_kernel, pairs, first, last, base),...]
    ppermute x0 -> x12, waiting for transfers between devices: none -> 16.3 us  [flip(): return lax.ppermute(block, axis, [(i, i ^ 1 << bit) for i in range(count)])]
    dot_general x1 -> x0, matrix products: 16.1 us -> none  [on_device(): jnp.dot(hidden, lax.all_gather(head, 'frames', axis=0, tiled=True), prefe...]
    ppermute x0 -> x12, starting transfers between devices: none -> 13.7 us  [flip(): return lax.ppermute(block, axis, [(i, i ^ 1 << bit) for i in range(count)])]
    reduce_sum x1 -> x0, other arithmetic: 8.7 us -> none  [on_device(): local_logit = jnp.sum(shifted * blocks, axis=2)]
    unnamed x0 -> x8, local copies, waits for them, and re-layouts: none -> 4.43 us
  transfers between devices with their start and end apart: 1 -> 12, of which waited for: 1 -> 5; matrix products, arithmetic and copies ran while one was open for 1% -> 2% of each run, Pallas kernels for 0% -> 22%
where the time goes in v1:
time: 56.1 us; the launch traced here: 55.9 us
  Pallas kernels  19.6 us (35%)
  waiting for transfers between devices  16.3 us (29%)
  starting transfers between devices  13.7 us (24%)
  local copies, waits for them, and re-layouts  5.49 us (10%)
  between operations  0.71 us (1%)
    ppermute x12, waiting for transfers between devices, flip(): return lax.ppermute(block, axis, [(i, i ^ 1 << bit) for i in range(count)])  16.3 us
    ppermute x12, starting transfers between devices, flip(): return lax.ppermute(block, axis, [(i, i ^ 1 << bit) for i in range(count)])  13.7 us
    pallas_call x2, Pallas kernels, chunk_stats(): pl.pallas_call(functools.partial(stats_kernel, pairs, first, last, base),...  12.2 us
    pallas_call x1, Pallas kernels, partial_logits(): pl.pallas_call(functools.partial(partial_kernel, widths), in_specs=[SMEM,...  6.08 us
    unnamed x8, local copies, waits for them, and re-layouts  4.43 us
    pallas_call x1, Pallas kernels, put_in_place(): pl.pallas_call(functools.partial(place_kernel, offsets), in_specs=[SMEM]...  1.3 us
  transfers between devices with their start and end apart: 12, of which 5 were waited for; matrix products, arithmetic and copies ran while one was open for 2% of the time, Pallas kernels for 22%

profile of v1, /device:TPU:0, one launch (start us, length us, event | category | flops | bytes accessed | tf_op | source)
XLA Modules:
  0.0 55.9 jit_solution(11673243990189498412)
XLA Ops:
  0.6 0.0 copy-start.2
  0.6 0.6 collective-permute-start
  1.2 1.1 %fusion = (bf16[256,512]{1,0:T(8,128)(2,1)S(1)}, bf16[256,512]{1,0:T(8,128)(2,1)S(1)}) fusion(bf16[256,1024]{1,0:T(8,128)(2,1)} %own.1), kind=kLoop, calls=%fused_computation.1 | loop fusion | bytes 1048576 | tf_op jit(solution)/shard_map/slice | solution.py:227
  2.3 2.6 %collective-permute-start.3 = (bf16[256,512]{1,0:T(8,128)(2,1)S(1)}, bf16[256,512]{1,0:T(8,128)(2,1)S(1)}, u32[]{:S(2)}, u32[]{:S(2)}) collective-permute-start(bf16[256,512]{1,0:T(8,128)(2,1)S(1)} %get-tuple-element.6), channel_id=1, source_target_pairs={{0,16},{8,24},{16,0},{24,8},{1,17},{9,25},{17,1},{25,9},{2,18},{10... | collective-permute-start | bytes 786440 | tf_op jit(solution)/shard_map/ppermute | solution.py:20
  4.8 0.1 collective-permute-start.1
  4.9 0.1 pad_add_fusion.place
  5.0 7.0 %collective-permute-done.3.rest_0_ = bf16[256,512]{1,0:T(8,128)(2,1)S(1)} collective-permute-done((bf16[256,512]{1,0:T(8,128)(2,1)S(1)}, bf16[256,512]{1,0:T(8,128)(2,1)S(1)}, u32[]{:S(2)}, u32[]{:S(2)}) %collective-permute-start.3) | collective-permute-done | bytes 262176 | tf_op jit(solution)/shard_map/ppermute | solution.py:20
  12.0 0.0 collective-permute-start.4
  12.0 5.4 %collective-permute-done.1.rest_0_ = bf16[256,512]{1,0:T(8,128)(2,1)S(1)} collective-permute-done((bf16[256,512]{1,0:T(8,128)(2,1)S(1)}, bf16[256,512]{1,0:T(8,128)(2,1)S(1)}, u32[]{:S(2)}, u32[]{:S(2)}) %collective-permute-start.1) | collective-permute-done | bytes 262176 | tf_op jit(solution)/shard_map/ppermute | solution.py:20
  17.4 0.0 collective-permute-start.2
  17.4 0.0 collective-permute-done.sibling
  17.4 0.0 copy-start
  17.4 3.4 %copy-done = bf16[4096,1024]{1,0:T(8,128)(2,1)S(1)} copy-done((bf16[4096,1024]{1,0:T(8,128)(2,1)S(1)}, bf16[4096,1024]{1,0:T(8,128)(2,1)}, u32[]{:S(2)}) %copy-start) | copy-done | bytes 8388632
  20.8 0.0 copy-start.3
  20.8 1.0 %copy-done.3 = bf16[256,1024]{1,0:T(8,128)(2,1)S(1)} copy-done((bf16[256,1024]{1,0:T(8,128)(2,1)S(1)}, bf16[256,1024]{1,0:T(8,128)(2,1)}, u32[]{:S(2)}) %copy-start.3) | copy-done | bytes 524312
  21.8 0.0 copy-start.1
  21.8 6.1 %partial.1 = (f32[512,4096]{1,0:T(8,128)S(1)}, f32[512,4096]{1,0:T(8,128)S(1)}) custom-call(s32[4]{0:T(128)S(1)} %pad_add_fusion.place, bf16[4096,1024]{1,0:T(8,128)(2,1)S(1)} %copy-done, bf16[256,1024]{1,0:T(8,128)(2,1)S(1)} %copy-done.3, bf16[256,1024]{1,0:T(8,128)(2,1)S(1)} %collective-permute-done.sibling), custom_call_target="tpu_custom_call" | custom-call | flops 4294967296 | bytes 1048576 | tf_op jit(solution)/shard_map/partial/pallas_call | solution.py:64
  27.9 0.0 collective-permute-done.4.rest_1_
  27.9 0.0 copy-done.2
  27.9 0.0 copy-done.1
  28.0 6.1 %stats.2.rest_2_ = f32[4,4096]{1,0:T(4,128)S(1)} custom-call(s32[4]{0:T(128)S(1)} %pad_add_fusion.place, bf16[4096,1024]{1,0:T(8,128)(2,1)S(1)} %copy-done.1, f32[512,4096]{1,0:T(8,128)S(1)} %get-tuple-element.5.part, s32[8,4096]{1,0:T(8,128)S(1)} %copy-done.2, bf16[256,512]{1,0:T(8,128)(2,1)S(1)} %collective-permute-done.3.rest_0_, ...), custom_call_target="tpu_custom_call" | custom-call | flops 2147483648 | bytes 1048576 | tf_op jit(solution)/shard_map/stats/pallas_call | solution.py:145
  34.0 0.0 collective-permute-done.2.rest_1_
  34.1 6.1 %stats.3.refs_0_ = f32[2,4096]{1,0:T(2,128)S(1)} custom-call(s32[4]{0:T(128)S(1)} %pad_add_fusion.place, bf16[4096,1024]{1,0:T(8,128)(2,1)S(1)} %copy-done.1, f32[512,4096]{1,0:T(8,128)S(1)} %get-tuple-element.4.part, s32[8,4096]{1,0:T(8,128)S(1)} %copy-done.2, bf16[256,512]{1,0:T(8,128)(2,1)S(1)} %collective-permute-done.1.rest_0_, ...), custom_call_target="tpu_custom_call" | custom-call | flops 2147483648 | bytes 1048576 | tf_op jit(solution)/shard_map/stats/pallas_call | solution.py:145
  40.2 2.9 %collective-permute-start.8 = (f32[2,4096]{1,0:T(2,128)S(1)}, f32[2,4096]{1,0:T(2,128)S(1)}, u32[]{:S(2)}, u32[]{:S(2)}) collective-permute-start(f32[2,4096]{1,0:T(2,128)S(1)} %stats.3.refs_0_), channel_id=1, source_target_pairs={{0,4},{1,5},{2,6},{3,7},{4,0},{5,1},{6,2},{7,3},{8,12},{9,13},{10,... | collective-permute-start | bytes 98312 | tf_op jit(solution)/shard_map/ppermute | solution.py:20
  43.1 1.6 %collective-permute-start.6 = (f32[2,4096]{1,0:T(2,128)S(1)}, f32[2,4096]{1,0:T(2,128)S(1)}, u32[]{:S(2)}, u32[]{:S(2)}) collective-permute-start(f32[2,4096]{1,0:T(2,128)S(1)} %stats.3.refs_0_), channel_id=1, source_target_pairs={{0,2},{1,3},{2,0},{3,1},{4,6},{5,7},{6,4},{7,5},{8,10},{9,11},{10,... | collective-permute-start | bytes 98312 | tf_op jit(solution)/shard_map/ppermute | solution.py:20
  44.7 0.5 collective-permute-done.8.refs_4_
  45.2 2.0 %collective-permute-start.10 = (f32[2,4096]{1,0:T(2,128)S(1)}, f32[2,4096]{1,0:T(2,128)S(1)}, u32[]{:S(2)}, u32[]{:S(2)}) collective-permute-start(f32[2,4096]{1,0:T(2,128)S(1)} %collective-permute-done.8.refs_4_), channel_id=1, source_target_pairs={{0,2},{1,3},{2,0},{3,1},{4,6},{5,7},{6,4},{7,5},{8,10},{9,11},{10,... | collective-permute-start | bytes 98312 | tf_op jit(solution)/shard_map/ppermute | solution.py:20
  47.2 1.5 %collective-permute-start.5 = (f32[2,4096]{1,0:T(2,128)S(1)}, f32[2,4096]{1,0:T(2,128)S(1)}, u32[]{:S(2)}, u32[]{:S(2)}) collective-permute-start(f32[2,4096]{1,0:T(2,128)S(1)} %stats.3.refs_0_), channel_id=1, source_target_pairs={{0,1},{1,0},{2,3},{3,2},{4,5},{5,4},{6,7},{7,6},{8,9},{9,8},{10,11... | collective-permute-start | bytes 98312 | tf_op jit(solution)/shard_map/ppermute | solution.py:20
  48.7 0.5 collective-permute-start.9
  49.2 0.0 collective-permute-done.6.refs_2_
  49.2 1.5 %collective-permute-start.7 = (f32[2,4096]{1,0:T(2,128)S(1)}, f32[2,4096]{1,0:T(2,128)S(1)}, u32[]{:S(2)}, u32[]{:S(2)}) collective-permute-start(f32[2,4096]{1,0:T(2,128)S(1)} %collective-permute-done.6.refs_2_), channel_id=1, source_target_pairs={{0,1},{1,0},{2,3},{3,2},{4,5},{5,4},{6,7},{7,6},{8,9},{9,8},{10,11... | collective-permute-start | bytes 98312 | tf_op jit(solution)/shard_map/ppermute | solution.py:20
  50.7 0.0 collective-permute-done.10.refs_6_
  50.7 0.5 collective-permute-start.11
  51.2 0.0 collective-permute-done.5.refs_1_
  51.2 1.9 %collective-permute-done.7.refs_3_ = f32[2,4096]{1,0:T(2,128)S(1)} collective-permute-done((f32[2,4096]{1,0:T(2,128)S(1)}, f32[2,4096]{1,0:T(2,128)S(1)}, u32[]{:S(2)}, u32[]{:S(2)}) %collective-permute-start.7) | collective-permute-done | bytes 32800 | tf_op jit(solution)/shard_map/ppermute | solution.py:20
  53.1 0.0 collective-permute-done.9.refs_5_
  53.1 1.5 %collective-permute-done.11.refs_7_ = f32[2,4096]{1,0:T(2,128)S(1)} collective-permute-done((f32[2,4096]{1,0:T(2,128)S(1)}, f32[2,4096]{1,0:T(2,128)S(1)}, u32[]{:S(2)}, u32[]{:S(2)}) %collective-permute-start.11) | collective-permute-done | bytes 32800 | tf_op jit(solution)/shard_map/ppermute | solution.py:20
  54.6 1.3 %place.1 = (f32[8,4096]{1,0:T(8,128)}, f32[8,4096]{1,0:T(8,128)}) custom-call(s32[4]{0:T(128)S(1)} %pad_add_fusion.place, f32[2,4096]{1,0:T(2,128)S(1)} %stats.3.refs_0_, f32[2,4096]{1,0:T(2,128)S(1)} %collective-permute-done.5.refs_1_, f32[2,4096]{1,0:T(2,128)S(1)} %collective-permute-done.6.refs_2_, f32[2,4096]{1,0:T(2,128)S(1)} %collective-permute-done.7.refs_3_, ...), custom_call_target="tpu_custom_call" | custom-call | tf_op jit(solution)/shard_map/place/pallas_call | solution.py:172
Async XLA Ops:
  0.6 27.3 %copy-start.2 = (s32[8,4096]{1,0:T(8,128)S(1)}, s32[8,4096]{1,0:T(8,128)}, u32[]{:S(2)}) copy-start(s32[8,4096]{1,0:T(8,128)} %chosen.3) | copy-start | bytes 393220
  0.6 16.8 %collective-permute-start = (bf16[256,1024]{1,0:T(8,128)(2,1)}, bf16[256,1024]{1,0:T(8,128)(2,1)S(1)}, u32[]{:S(2)}, u32[]{:S(2)}) collective-permute-start(bf16[256,1024]{1,0:T(8,128)(2,1)} %own.1), channel_id=1, source_target_pairs={{0,8},{8,0},{16,24},{24,16},{1,9},{9,1},{17,25},{25,17},{2,10},{10... | collective-permute-start | bytes 1572872 | tf_op jit(solution)/shard_map/ppermute | solution.py:20
  2.3 9.7 %collective-permute-start.3 = (bf16[256,512]{1,0:T(8,128)(2,1)S(1)}, bf16[256,512]{1,0:T(8,128)(2,1)S(1)}, u32[]{:S(2)}, u32[]{:S(2)}) collective-permute-start(bf16[256,512]{1,0:T(8,128)(2,1)S(1)} %get-tuple-element.6), channel_id=1, source_target_pairs={{0,16},{8,24},{16,0},{24,8},{1,17},{9,25},{17,1},{25,9},{2,18},{10... | collective-permute-start | bytes 786440 | tf_op jit(solution)/shard_map/ppermute | solution.py:20
  4.8 12.6 %collective-permute-start.1 = (bf16[256,512]{1,0:T(8,128)(2,1)S(1)}, bf16[256,512]{1,0:T(8,128)(2,1)S(1)}, u32[]{:S(2)}, u32[]{:S(2)}) collective-permute-start(bf16[256,512]{1,0:T(8,128)(2,1)S(1)} %get-tuple-element.7), channel_id=1, source_target_pairs={{0,16},{8,24},{16,0},{24,8},{1,17},{9,25},{17,1},{25,9},{2,18},{10... | collective-permute-start | bytes 786440 | tf_op jit(solution)/shard_map/ppermute | solution.py:20
  12.0 16.0 %collective-permute-start.4 = (bf16[256,512]{1,0:T(8,128)(2,1)S(1)}, bf16[256,512]{1,0:T(8,128)(2,1)S(1)}, u32[]{:S(2)}, u32[]{:S(2)}) collective-permute-start(bf16[256,512]{1,0:T(8,128)(2,1)S(1)} %collective-permute-done.3.rest_0_), channel_id=1, source_target_pairs={{0,8},{8,0},{16,24},{24,16},{1,9},{9,1},{17,25},{25,17},{2,10},{10... | collective-permute-start | bytes 786440 | tf_op jit(solution)/shard_map/ppermute | solution.py:20
  17.4 16.6 %collective-permute-start.2 = (bf16[256,512]{1,0:T(8,128)(2,1)S(1)}, bf16[256,512]{1,0:T(8,128)(2,1)S(1)}, u32[]{:S(2)}, u32[]{:S(2)}) collective-permute-start(bf16[256,512]{1,0:T(8,128)(2,1)S(1)} %collective-permute-done.1.rest_0_), channel_id=1, source_target_pairs={{0,8},{8,0},{16,24},{24,16},{1,9},{9,1},{17,25},{25,17},{2,10},{10... | collective-permute-start | bytes 786440 | tf_op jit(solution)/shard_map/ppermute | solution.py:20
  17.4 3.4 %copy-start = (bf16[4096,1024]{1,0:T(8,128)(2,1)S(1)}, bf16[4096,1024]{1,0:T(8,128)(2,1)}, u32[]{:S(2)}) copy-start(bf16[4096,1024]{1,0:T(8,128)(2,1)} %hidden.5) | copy-start | bytes 25165828
  20.8 1.0 %copy-start.3 = (bf16[256,1024]{1,0:T(8,128)(2,1)S(1)}, bf16[256,1024]{1,0:T(8,128)(2,1)}, u32[]{:S(2)}) copy-start(bf16[256,1024]{1,0:T(8,128)(2,1)} %own.1) | copy-start | bytes 1572868
  21.8 6.1 %copy-start.1 = (bf16[4096,1024]{1,0:T(8,128)(2,1)S(1)}, bf16[4096,1024]{1,0:T(8,128)(2,1)}, u32[]{:S(2)}) copy-start(bf16[4096,1024]{1,0:T(8,128)(2,1)} %hidden.5) | copy-start | bytes 25165828
  40.2 5.0 %collective-permute-start.8 = (f32[2,4096]{1,0:T(2,128)S(1)}, f32[2,4096]{1,0:T(2,128)S(1)}, u32[]{:S(2)}, u32[]{:S(2)}) collective-permute-start(f32[2,4096]{1,0:T(2,128)S(1)} %stats.3.refs_0_), channel_id=1, source_target_pairs={{0,4},{1,5},{2,6},{3,7},{4,0},{5,1},{6,2},{7,3},{8,12},{9,13},{10,... | collective-permute-start | bytes 98312 | tf_op jit(solution)/shard_map/ppermute | solution.py:20
  43.1 6.0 %collective-permute-start.6 = (f32[2,4096]{1,0:T(2,128)S(1)}, f32[2,4096]{1,0:T(2,128)S(1)}, u32[]{:S(2)}, u32[]{:S(2)}) collective-permute-start(f32[2,4096]{1,0:T(2,128)S(1)} %stats.3.refs_0_), channel_id=1, source_target_pairs={{0,2},{1,3},{2,0},{3,1},{4,6},{5,7},{6,4},{7,5},{8,10},{9,11},{10,... | collective-permute-start | bytes 98312 | tf_op jit(solution)/shard_map/ppermute | solution.py:20
  45.2 5.5 %collective-permute-start.10 = (f32[2,4096]{1,0:T(2,128)S(1)}, f32[2,4096]{1,0:T(2,128)S(1)}, u32[]{:S(2)}, u32[]{:S(2)}) collective-permute-start(f32[2,4096]{1,0:T(2,128)S(1)} %collective-permute-done.8.refs_4_), channel_id=1, source_target_pairs={{0,2},{1,3},{2,0},{3,1},{4,6},{5,7},{6,4},{7,5},{8,10},{9,11},{10,... | collective-permute-start | bytes 98312 | tf_op jit(solution)/shard_map/ppermute | solution.py:20
  47.2 4.1 %collective-permute-start.5 = (f32[2,4096]{1,0:T(2,128)S(1)}, f32[2,4096]{1,0:T(2,128)S(1)}, u32[]{:S(2)}, u32[]{:S(2)}) collective-permute-start(f32[2,4096]{1,0:T(2,128)S(1)} %stats.3.refs_0_), channel_id=1, source_target_pairs={{0,1},{1,0},{2,3},{3,2},{4,5},{5,4},{6,7},{7,6},{8,9},{9,8},{10,11... | collective-permute-start | bytes 98312 | tf_op jit(solution)/shard_map/ppermute | solution.py:20
  48.7 4.4 %collective-permute-start.9 = (f32[2,4096]{1,0:T(2,128)S(1)}, f32[2,4096]{1,0:T(2,128)S(1)}, u32[]{:S(2)}, u32[]{:S(2)}) collective-permute-start(f32[2,4096]{1,0:T(2,128)S(1)} %collective-permute-done.8.refs_4_), channel_id=1, source_target_pairs={{0,1},{1,0},{2,3},{3,2},{4,5},{5,4},{6,7},{7,6},{8,9},{9,8},{10,11... | collective-permute-start | bytes 98312 | tf_op jit(solution)/shard_map/ppermute | solution.py:20
  49.2 3.9 %collective-permute-start.7 = (f32[2,4096]{1,0:T(2,128)S(1)}, f32[2,4096]{1,0:T(2,128)S(1)}, u32[]{:S(2)}, u32[]{:S(2)}) collective-permute-start(f32[2,4096]{1,0:T(2,128)S(1)} %collective-permute-done.6.refs_2_), channel_id=1, source_target_pairs={{0,1},{1,0},{2,3},{3,2},{4,5},{5,4},{6,7},{7,6},{8,9},{9,8},{10,11... | collective-permute-start | bytes 98312 | tf_op jit(solution)/shard_map/ppermute | solution.py:20
  50.7 3.9 %collective-permute-start.11 = (f32[2,4096]{1,0:T(2,128)S(1)}, f32[2,4096]{1,0:T(2,128)S(1)}, u32[]{:S(2)}, u32[]{:S(2)}) collective-permute-start(f32[2,4096]{1,0:T(2,128)S(1)} %collective-permute-done.10.refs_6_), channel_id=1, source_target_pairs={{0,1},{1,0},{2,3},{3,2},{4,5},{5,4},{6,7},{7,6},{8,9},{9,8},{10,11... | collective-permute-start | bytes 98312 | tf_op jit(solution)/shard_map/ppermute | solution.py:20
